TPU v7x, 32 devices: a whole 2x2x4 slice. The times are simulated.
32 devices in a mesh: scen: 8 (over y, x, core), veh: 4 (over z).
Axes of the slice: x: 2, y: 2, z: 4, core: 2. Of those that a mesh axis runs over, the one named last changes fastest.
Arguments:
- start_plan: bfloat16 [128, 3584, 128], P('scen', 'veh'), may hold values from -6 to 6
- linear_cost: bfloat16 [128, 3584, 128], P('scen', 'veh'), may hold values from -12 to 12
- price: bfloat16 [128, 3584, 128], P('scen', 'veh'), may hold values from -6 to 6
- anchor: bfloat16 [8, 3584, 128], P(None, 'veh'), may hold values from -6 to 6
- hessian: bfloat16 [128, 128, 128], P('scen'), as said below
- usage_coef: bfloat16 [3584, 128], P('veh'), may hold values from -1.5 to 1.5
- crew_limit: float32 [128, 350], P('scen'), may hold values from -48 to 48
- crew_dual: float32 [128, 350], P('scen'), may hold values from 0 to 2
- crew_row: int32 [3584], P('veh'), may hold values from 0 to 349
- bundle_of: int32 [128, 1], replicated, may hold values from 0 to 7
- scen_weight: int32 [128], replicated, may hold values from 1 to 8
Outputs:
- new_plan: bfloat16 [128, 3584, 128], P('scen', 'veh')
- new_price: bfloat16 [128, 3584, 128], P('scen', 'veh')
- bundle_mean: bfloat16 [8, 3584, 128], P('scen', 'veh')
- new_dual: float32 [128, 350], P('scen')
- gap: float32 [], replicated
Inputs may be any that keep to these rules, and one draw needn't show every extreme that they name: `bundle_of`: every bundle holds one scenario or more. `hessian`: symmetric.
All inputs are finite; a program needn't handle non-finite values.
Results may differ from a plain program's by a relative error of at most 0.0013.
The roundings to bfloat16 on the way count: a program that leaves them out, or rounds other values in their place, can miss the bound.
Values sent between devices are 32-bit elements; how exact they have to be, the bound alone decides.
A program may use at most 128 MiB of HBM per device.

v0:
```python
import jax
import jax.numpy as jnp
from jax import lax
from jax.sharding import PartitionSpec as P

ITERS = 12
penalty = 1.0
step_size = 0.02
dual_step = 0.02
highest = lax.Precision.HIGHEST


def shards(
    start_plan,
    linear_cost,
    price,
    anchor,
    hessian,
    usage_coef,
    crew_limit,
    crew_dual,
    crew_row,
    bundle_of,
    scen_weight,
):
    local_scen = start_plan.shape[0]
    bundle_count = anchor.shape[0]
    crew_count = crew_limit.shape[1]
    offset = lax.axis_index("scen") * local_scen
    all_bundles = bundle_of[:, 0]
    my_bundles = lax.dynamic_slice_in_dim(all_bundles, offset, local_scen)
    my_weights = lax.dynamic_slice_in_dim(scen_weight, offset, local_scen).astype(jnp.float32)
    bundle_ids = jnp.arange(bundle_count, dtype=jnp.int32)
    selector = (my_bundles[:, None] == bundle_ids[None, :]).astype(jnp.float32)
    anchored = jnp.einsum(
        "sb,bvi->svi", selector.astype(jnp.bfloat16), anchor, preferred_element_type=jnp.float32
    )
    linear_part = linear_cost.astype(jnp.float32) + price.astype(jnp.float32) - penalty * anchored
    coefficient = usage_coef.astype(jnp.float32)
    crew_map = (crew_row[:, None] == jnp.arange(crew_count, dtype=jnp.int32)[None, :]).astype(
        jnp.float32
    )

    def advance(index, state_pair):
        roster, multiplier = state_pair
        rounded = roster.astype(jnp.bfloat16)
        curvature = jnp.einsum("svi,sij->svj", rounded, hessian, preferred_element_type=jnp.float32)
        consumed = jnp.sum(roster * coefficient[None], axis=2)
        partial_use = jnp.dot(consumed, crew_map, precision=highest)
        usage = lax.psum(partial_use, "veh")
        updated = jnp.maximum(multiplier + dual_step * (usage - crew_limit), 0.0)
        per_vehicle = jnp.dot(multiplier, crew_map.T, precision=highest)
        gradient = (
            curvature + linear_part + penalty * roster + per_vehicle[:, :, None] * coefficient[None]
        )
        return (roster - step_size * gradient, updated)

    roster, multiplier = lax.fori_loop(
        0, ITERS, advance, (start_plan.astype(jnp.float32), crew_dual)
    )
    weighted_pick = selector * my_weights[:, None]
    every_weight = jnp.sum(
        (all_bundles[:, None] == bundle_ids[None, :]).astype(jnp.float32)
        * scen_weight.astype(jnp.float32)[:, None],
        axis=0,
    )
    owned_rows = bundle_count // lax.axis_size("scen")
    own_start = lax.axis_index("scen") * owned_rows
    partial_sums = jnp.einsum("sb,svi->bvi", weighted_pick, roster, precision=highest)
    totals = lax.psum(partial_sums, "scen")
    every_mean = totals / every_weight[:, None, None]
    own_mean = lax.dynamic_slice_in_dim(every_mean, own_start, owned_rows)
    mean_here = jnp.einsum("sb,bvi->svi", selector, every_mean, precision=highest)
    deviation = roster - mean_here
    new_price = (price.astype(jnp.float32) + penalty * deviation).astype(jnp.bfloat16)
    spread = jnp.sum(my_weights * jnp.sum(deviation * deviation, axis=(1, 2)))
    spread_total = lax.psum(spread, ("scen", "veh"))
    entries = start_plan.shape[1] * lax.axis_size("veh") * start_plan.shape[2]
    gap = jnp.sqrt(spread_total / (jnp.sum(scen_weight.astype(jnp.float32)) * entries))
    return (roster.astype(jnp.bfloat16), new_price, own_mean.astype(jnp.bfloat16), multiplier, gap)


def solution(mesh):
    return jax.shard_map(
        shards,
        mesh=mesh,
        in_specs=(
            P("scen", "veh", None),
            P("scen", "veh", None),
            P("scen", "veh", None),
            P(None, "veh", None),
            P("scen", None, None),
            P("veh", None),
            P("scen", None),
            P("scen", None),
            P("veh"),
            P(),
            P(),
        ),
        out_specs=(
            P("scen", "veh", None),
            P("scen", "veh", None),
            P("scen", "veh", None),
            P("scen", None),
            P(),
        ),
        check_vma=False,
    )
```

profile of v0, /device:TPU:0, one launch (start us, length us, event | category | flops | bytes accessed | tf_op | source)
XLA Modules:
  0.0 568.2 jit_solution(2180171724463665782)
XLA Ops:
  8.7 22.6 %fusion.12 = f32[16,896,128]{2,0,1:T(8,128)S(1)} fusion(bf16[16,896,128]{2,1,0:T(8,128)(2,1)} %param.14, bf16[16,896,128]{2,1,0:T(8,128)(2,1)} %param.15, bf16[8,896,128]{2,1,0:T(8,128)(2,1)S(1)} %copy-done, s32[16]{0:T(128)S(1)} %dynamic-slice_bitcast_fusion), kind=kOutput, calls=%fused_computation.15 | convolution fusion | flops 36700544 | bytes 16515136 | tf_op jit(solution)/shard_map/sb,bvi->svi/dot_general | solution.py:35
  31.3 5.2 copy.27
  36.5 3.8 convert_element_type.42
  40.4 364.3 %while.13 = (s32[]{:T(128)}, f32[16,896,128]{2,1,0:T(8,128)}, f32[16,350]{1,0:T(8,128)S(1)}, bf16[16,128,128]{2,1,0:T(8,128)(2,1)S(1)}, f32[16,896,128]{2,1,0:T(...) while((s32[]{:T(128)}, f32[16,896,128]{2,1,0:T(8,128)}, ...), condition=%wide.region_3.0_spmd.clone, body=%wide.region_0.0_spmd.clone.sunk | while | flops 607967616 | bytes 75257976 | solution.py:58
  40.4 3.1 copy.53
  47.0 5.9 %multiply_subtract_fusion.2 = f32[16,896,128]{2,1,0:T(8,128)} fusion(f32[16,896,128]{2,1,0:T(8,128)S(1)} %copy.53, f32[16,896,128]{2,1,0:T(8,128)S(1)} %copy-done.1, f32[896,128]{1,0:T(8,128)S(1)} %get-tuple-element.185, f32[16,896]{1,0:T(8,128)S(1)} %fusion.47, bf16[16,128,128]{2,1,0:T(8,128)(2,1)S(1)} %get-tuple-element.183), kind=kOutput, calls=%fused_computation.2.clone.1 | convolution fusion | flops 482607104 | bytes 23060480 | tf_op jit(solution)/shard_map/while/body/eval_jaxpr/svi,sij->svj/dot_general | solution.py:47
  53.8 20.8 %psum.25 = f32[16,350]{1,0:T(8,128)S(1)} all-reduce(f32[16,350]{1,0:T(8,128)S(1)} %fusion.48), channel_id=1, replica_groups=mesh['scen'=8,'veh'=4] {'veh'}, use_global_device_ids=true, to_apply=%region_2.0 | all-reduce | flops 5600 | bytes 44800 | tf_op jit(solution)/shard_map/while/body/eval_jaxpr/psum | solution.py:50
  74.6 3.1 copy.53
  81.1 5.9 %multiply_subtract_fusion.2 = f32[16,896,128]{2,1,0:T(8,128)} fusion(f32[16,896,128]{2,1,0:T(8,128)S(1)} %copy.53, f32[16,896,128]{2,1,0:T(8,128)S(1)} %copy-done.1, f32[896,128]{1,0:T(8,128)S(1)} %get-tuple-element.185, f32[16,896]{1,0:T(8,128)S(1)} %fusion.47, bf16[16,128,128]{2,1,0:T(8,128)(2,1)S(1)} %get-tuple-element.183), kind=kOutput, calls=%fused_computation.2.clone.1 | convolution fusion | flops 482607104 | bytes 23060480 | tf_op jit(solution)/shard_map/while/body/eval_jaxpr/svi,sij->svj/dot_general | solution.py:47
  88.0 15.8 %psum.25 = f32[16,350]{1,0:T(8,128)S(1)} all-reduce(f32[16,350]{1,0:T(8,128)S(1)} %fusion.48), channel_id=1, replica_groups=mesh['scen'=8,'veh'=4] {'veh'}, use_global_device_ids=true, to_apply=%region_2.0 | all-reduce | flops 5600 | bytes 44800 | tf_op jit(solution)/shard_map/while/body/eval_jaxpr/psum | solution.py:50
  103.8 3.1 copy.53
  110.4 5.9 %multiply_subtract_fusion.2 = f32[16,896,128]{2,1,0:T(8,128)} fusion(f32[16,896,128]{2,1,0:T(8,128)S(1)} %copy.53, f32[16,896,128]{2,1,0:T(8,128)S(1)} %copy-done.1, f32[896,128]{1,0:T(8,128)S(1)} %get-tuple-element.185, f32[16,896]{1,0:T(8,128)S(1)} %fusion.47, bf16[16,128,128]{2,1,0:T(8,128)(2,1)S(1)} %get-tuple-element.183), kind=kOutput, calls=%fused_computation.2.clone.1 | convolution fusion | flops 482607104 | bytes 23060480 | tf_op jit(solution)/shard_map/while/body/eval_jaxpr/svi,sij->svj/dot_general | solution.py:47
  117.2 17.4 %psum.25 = f32[16,350]{1,0:T(8,128)S(1)} all-reduce(f32[16,350]{1,0:T(8,128)S(1)} %fusion.48), channel_id=1, replica_groups=mesh['scen'=8,'veh'=4] {'veh'}, use_global_device_ids=true, to_apply=%region_2.0 | all-reduce | flops 5600 | bytes 44800 | tf_op jit(solution)/shard_map/while/body/eval_jaxpr/psum | solution.py:50
  134.7 3.1 copy.53
  141.2 5.9 %multiply_subtract_fusion.2 = f32[16,896,128]{2,1,0:T(8,128)} fusion(f32[16,896,128]{2,1,0:T(8,128)S(1)} %copy.53, f32[16,896,128]{2,1,0:T(8,128)S(1)} %copy-done.1, f32[896,128]{1,0:T(8,128)S(1)} %get-tuple-element.185, f32[16,896]{1,0:T(8,128)S(1)} %fusion.47, bf16[16,128,128]{2,1,0:T(8,128)(2,1)S(1)} %get-tuple-element.183), kind=kOutput, calls=%fused_computation.2.clone.1 | convolution fusion | flops 482607104 | bytes 23060480 | tf_op jit(solution)/shard_map/while/body/eval_jaxpr/svi,sij->svj/dot_general | solution.py:47
  148.1 15.8 %psum.25 = f32[16,350]{1,0:T(8,128)S(1)} all-reduce(f32[16,350]{1,0:T(8,128)S(1)} %fusion.48), channel_id=1, replica_groups=mesh['scen'=8,'veh'=4] {'veh'}, use_global_device_ids=true, to_apply=%region_2.0 | all-reduce | flops 5600 | bytes 44800 | tf_op jit(solution)/shard_map/while/body/eval_jaxpr/psum | solution.py:50
  163.9 3.1 copy.53
  170.5 5.9 %multiply_subtract_fusion.2 = f32[16,896,128]{2,1,0:T(8,128)} fusion(f32[16,896,128]{2,1,0:T(8,128)S(1)} %copy.53, f32[16,896,128]{2,1,0:T(8,128)S(1)} %copy-done.1, f32[896,128]{1,0:T(8,128)S(1)} %get-tuple-element.185, f32[16,896]{1,0:T(8,128)S(1)} %fusion.47, bf16[16,128,128]{2,1,0:T(8,128)(2,1)S(1)} %get-tuple-element.183), kind=kOutput, calls=%fused_computation.2.clone.1 | convolution fusion | flops 482607104 | bytes 23060480 | tf_op jit(solution)/shard_map/while/body/eval_jaxpr/svi,sij->svj/dot_general | solution.py:47
  177.3 17.4 %psum.25 = f32[16,350]{1,0:T(8,128)S(1)} all-reduce(f32[16,350]{1,0:T(8,128)S(1)} %fusion.48), channel_id=1, replica_groups=mesh['scen'=8,'veh'=4] {'veh'}, use_global_device_ids=true, to_apply=%region_2.0 | all-reduce | flops 5600 | bytes 44800 | tf_op jit(solution)/shard_map/while/body/eval_jaxpr/psum | solution.py:50
  194.8 3.1 copy.53
  201.3 5.9 %multiply_subtract_fusion.2 = f32[16,896,128]{2,1,0:T(8,128)} fusion(f32[16,896,128]{2,1,0:T(8,128)S(1)} %copy.53, f32[16,896,128]{2,1,0:T(8,128)S(1)} %copy-done.1, f32[896,128]{1,0:T(8,128)S(1)} %get-tuple-element.185, f32[16,896]{1,0:T(8,128)S(1)} %fusion.47, bf16[16,128,128]{2,1,0:T(8,128)(2,1)S(1)} %get-tuple-element.183), kind=kOutput, calls=%fused_computation.2.clone.1 | convolution fusion | flops 482607104 | bytes 23060480 | tf_op jit(solution)/shard_map/while/body/eval_jaxpr/svi,sij->svj/dot_general | solution.py:47
  208.2 16.0 %psum.25 = f32[16,350]{1,0:T(8,128)S(1)} all-reduce(f32[16,350]{1,0:T(8,128)S(1)} %fusion.48), channel_id=1, replica_groups=mesh['scen'=8,'veh'=4] {'veh'}, use_global_device_ids=true, to_apply=%region_2.0 | all-reduce | flops 5600 | bytes 44800 | tf_op jit(solution)/shard_map/while/body/eval_jaxpr/psum | solution.py:50
  224.2 3.1 copy.53
  230.7 5.9 %multiply_subtract_fusion.2 = f32[16,896,128]{2,1,0:T(8,128)} fusion(f32[16,896,128]{2,1,0:T(8,128)S(1)} %copy.53, f32[16,896,128]{2,1,0:T(8,128)S(1)} %copy-done.1, f32[896,128]{1,0:T(8,128)S(1)} %get-tuple-element.185, f32[16,896]{1,0:T(8,128)S(1)} %fusion.47, bf16[16,128,128]{2,1,0:T(8,128)(2,1)S(1)} %get-tuple-element.183), kind=kOutput, calls=%fused_computation.2.clone.1 | convolution fusion | flops 482607104 | bytes 23060480 | tf_op jit(solution)/shard_map/while/body/eval_jaxpr/svi,sij->svj/dot_general | solution.py:47
  237.5 17.3 %psum.25 = f32[16,350]{1,0:T(8,128)S(1)} all-reduce(f32[16,350]{1,0:T(8,128)S(1)} %fusion.48), channel_id=1, replica_groups=mesh['scen'=8,'veh'=4] {'veh'}, use_global_device_ids=true, to_apply=%region_2.0 | all-reduce | flops 5600 | bytes 44800 | tf_op jit(solution)/shard_map/while/body/eval_jaxpr/psum | solution.py:50
  254.9 3.1 copy.53
  261.4 5.9 %multiply_subtract_fusion.2 = f32[16,896,128]{2,1,0:T(8,128)} fusion(f32[16,896,128]{2,1,0:T(8,128)S(1)} %copy.53, f32[16,896,128]{2,1,0:T(8,128)S(1)} %copy-done.1, f32[896,128]{1,0:T(8,128)S(1)} %get-tuple-element.185, f32[16,896]{1,0:T(8,128)S(1)} %fusion.47, bf16[16,128,128]{2,1,0:T(8,128)(2,1)S(1)} %get-tuple-element.183), kind=kOutput, calls=%fused_computation.2.clone.1 | convolution fusion | flops 482607104 | bytes 23060480 | tf_op jit(solution)/shard_map/while/body/eval_jaxpr/svi,sij->svj/dot_general | solution.py:47
  268.3 16.1 %psum.25 = f32[16,350]{1,0:T(8,128)S(1)} all-reduce(f32[16,350]{1,0:T(8,128)S(1)} %fusion.48), channel_id=1, replica_groups=mesh['scen'=8,'veh'=4] {'veh'}, use_global_device_ids=true, to_apply=%region_2.0 | all-reduce | flops 5600 | bytes 44800 | tf_op jit(solution)/shard_map/while/body/eval_jaxpr/psum | solution.py:50
  284.4 3.1 copy.53
  291.0 5.9 %multiply_subtract_fusion.2 = f32[16,896,128]{2,1,0:T(8,128)} fusion(f32[16,896,128]{2,1,0:T(8,128)S(1)} %copy.53, f32[16,896,128]{2,1,0:T(8,128)S(1)} %copy-done.1, f32[896,128]{1,0:T(8,128)S(1)} %get-tuple-element.185, f32[16,896]{1,0:T(8,128)S(1)} %fusion.47, bf16[16,128,128]{2,1,0:T(8,128)(2,1)S(1)} %get-tuple-element.183), kind=kOutput, calls=%fused_computation.2.clone.1 | convolution fusion | flops 482607104 | bytes 23060480 | tf_op jit(solution)/shard_map/while/body/eval_jaxpr/svi,sij->svj/dot_general | solution.py:47
  297.8 17.1 %psum.25 = f32[16,350]{1,0:T(8,128)S(1)} all-reduce(f32[16,350]{1,0:T(8,128)S(1)} %fusion.48), channel_id=1, replica_groups=mesh['scen'=8,'veh'=4] {'veh'}, use_global_device_ids=true, to_apply=%region_2.0 | all-reduce | flops 5600 | bytes 44800 | tf_op jit(solution)/shard_map/while/body/eval_jaxpr/psum | solution.py:50
  315.0 3.1 copy.53
  321.5 5.9 %multiply_subtract_fusion.2 = f32[16,896,128]{2,1,0:T(8,128)} fusion(f32[16,896,128]{2,1,0:T(8,128)S(1)} %copy.53, f32[16,896,128]{2,1,0:T(8,128)S(1)} %copy-done.1, f32[896,128]{1,0:T(8,128)S(1)} %get-tuple-element.185, f32[16,896]{1,0:T(8,128)S(1)} %fusion.47, bf16[16,128,128]{2,1,0:T(8,128)(2,1)S(1)} %get-tuple-element.183), kind=kOutput, calls=%fused_computation.2.clone.1 | convolution fusion | flops 482607104 | bytes 23060480 | tf_op jit(solution)/shard_map/while/body/eval_jaxpr/svi,sij->svj/dot_general | solution.py:47
  328.4 16.2 %psum.25 = f32[16,350]{1,0:T(8,128)S(1)} all-reduce(f32[16,350]{1,0:T(8,128)S(1)} %fusion.48), channel_id=1, replica_groups=mesh['scen'=8,'veh'=4] {'veh'}, use_global_device_ids=true, to_apply=%region_2.0 | all-reduce | flops 5600 | bytes 44800 | tf_op jit(solution)/shard_map/while/body/eval_jaxpr/psum | solution.py:50
  344.6 3.1 copy.53
  351.1 5.9 %multiply_subtract_fusion.2 = f32[16,896,128]{2,1,0:T(8,128)} fusion(f32[16,896,128]{2,1,0:T(8,128)S(1)} %copy.53, f32[16,896,128]{2,1,0:T(8,128)S(1)} %copy-done.1, f32[896,128]{1,0:T(8,128)S(1)} %get-tuple-element.185, f32[16,896]{1,0:T(8,128)S(1)} %fusion.47, bf16[16,128,128]{2,1,0:T(8,128)(2,1)S(1)} %get-tuple-element.183), kind=kOutput, calls=%fused_computation.2.clone.1 | convolution fusion | flops 482607104 | bytes 23060480 | tf_op jit(solution)/shard_map/while/body/eval_jaxpr/svi,sij->svj/dot_general | solution.py:47
  358.0 17.1 %psum.25 = f32[16,350]{1,0:T(8,128)S(1)} all-reduce(f32[16,350]{1,0:T(8,128)S(1)} %fusion.48), channel_id=1, replica_groups=mesh['scen'=8,'veh'=4] {'veh'}, use_global_device_ids=true, to_apply=%region_2.0 | all-reduce | flops 5600 | bytes 44800 | tf_op jit(solution)/shard_map/while/body/eval_jaxpr/psum | solution.py:50
  375.1 3.1 copy.53
  381.6 5.9 %multiply_subtract_fusion.2 = f32[16,896,128]{2,1,0:T(8,128)} fusion(f32[16,896,128]{2,1,0:T(8,128)S(1)} %copy.53, f32[16,896,128]{2,1,0:T(8,128)S(1)} %copy-done.1, f32[896,128]{1,0:T(8,128)S(1)} %get-tuple-element.185, f32[16,896]{1,0:T(8,128)S(1)} %fusion.47, bf16[16,128,128]{2,1,0:T(8,128)(2,1)S(1)} %get-tuple-element.183), kind=kOutput, calls=%fused_computation.2.clone.1 | convolution fusion | flops 482607104 | bytes 23060480 | tf_op jit(solution)/shard_map/while/body/eval_jaxpr/svi,sij->svj/dot_general | solution.py:47
  388.5 16.2 %psum.25 = f32[16,350]{1,0:T(8,128)S(1)} all-reduce(f32[16,350]{1,0:T(8,128)S(1)} %fusion.48), channel_id=1, replica_groups=mesh['scen'=8,'veh'=4] {'veh'}, use_global_device_ids=true, to_apply=%region_2.0 | all-reduce | flops 5600 | bytes 44800 | tf_op jit(solution)/shard_map/while/body/eval_jaxpr/psum | solution.py:50
  404.8 14.0 %fusion.14 = f32[8,896,128]{2,0,1:T(8,128)} fusion(f32[16,896,128]{2,1,0:T(8,128)} %get-tuple-element.48, f32[16]{0:T(128)S(1)} %dynamic-slice_convert_fusion.1, s32[16]{0:T(128)S(1)} %dynamic-slice_bitcast_fusion), kind=kOutput, calls=%fused_computation.18 | convolution fusion | flops 176161024 | bytes 11010176 | tf_op jit(solution)/shard_map/sb,svi->bvi/dot_general | solution.py:69
  418.8 5.6 convert_element_type.49
  425.8 67.3 %all-reduce.2.cloned.1.call-done = f32[8,896,128]{2,0,1:T(8,128)} async-done(((f32[8,896,128]{2,0,1:T(8,128)}), f32[8,896,128]{2,0,1:T(8,128)}) %all-reduce.2.cloned.1.call-update) | async-done | bytes 3670032 | tf_op jit(solution)/shard_map/psum | solution.py:70
  493.1 2.5 broadcast_divide_fusion
  496.2 17.2 %multiply_reduce_fusion.1 = (f32[16]{0:T(128)S(1)}, bf16[16,896,128]{2,0,1:T(8,128)(2,1)S(1)}) fusion(bf16[16,896,128]{2,1,0:T(8,128)(2,1)S(1)} %copy-done.3, f32[8,896,128]{2,0,1:T(8,128)S(1)} %broadcast_divide_fusion, s32[16]{0:T(128)S(1)} %dynamic-slice_bitcast_fusion, f32[16,896,128]{2,1,0:T(8,128)} %get-tuple-element.48), kind=kOutput, calls=%fused_computation.17 | convolution fusion | flops 187170928 | bytes 18350208 | tf_op jit(solution)/shard_map/sb,bvi->svi/dot_general | solution.py:73
  514.1 2.8 copy.30
  516.9 39.5 %psum.22 = f32[]{:T(128)} all-reduce(f32[]{:T(128)} %multiply_reduce_fusion.2), channel_id=1, replica_groups=mesh['scen'=8,'veh'=4] {'scen','veh'}, use_global_device_ids=true, to_apply=%region_8.0 | all-reduce | flops 1 | bytes 8 | tf_op jit(solution)/shard_map/psum | solution.py:77
  557.1 2.4 dynamic-slice_convert_fusion
  (106 shorter events, 57.5 us)
Async XLA Ops:
  7.2 1.5 copy-start
  7.2 485.9 %all-reduce.2.cloned.1.call-start = ((), (), s32[]{:S(2)}) async-start(), calls=%async_computation | async-start | bytes 7340032 | tf_op jit(solution)/shard_map/psum | solution.py:70
  31.3 5.2 copy-start.5
  36.5 3.8 copy-start.9
  36.5 3.8 copy-start.4
  36.5 3.9 copy-start.7
  36.5 3.9 copy-start.8
  36.5 3.9 copy-start.11
  40.4 364.3 %copy-start.10 = (s32[128]{0:T(128)S(1)}, s32[128]{0:T(128)}, u32[]{:S(2)}) copy-start(s32[128]{0:T(128)} %param.23) | copy-start | bytes 1540
  43.5 3.5 copy-start.1
  77.7 3.5 copy-start.1
  106.9 3.5 copy-start.1
  137.8 3.5 copy-start.1
  167.0 3.5 copy-start.1
  197.9 3.5 copy-start.1
  227.2 3.5 copy-start.1
  258.0 3.5 copy-start.1
  287.5 3.5 copy-start.1
  318.1 3.5 copy-start.1
  347.7 3.5 copy-start.1
  378.1 3.5 copy-start.1
  404.7 14.1 %copy-start.6 = (f32[16,350]{1,0:T(8,128)}, f32[16,350]{1,0:T(8,128)S(1)}, u32[]{:S(2)}) copy-start(f32[16,350]{1,0:T(8,128)S(1)} %get-tuple-element.93) | copy-start | bytes 67204
  418.7 6.9 %copy-start.12 = (s32[128,1]{0,1:T(1,128)S(1)}, s32[128,1]{0,1:T(1,128)}, u32[]{:S(2)}) copy-start(s32[128,1]{0,1:T(1,128)} %param.22) | copy-start | bytes 1540
  493.1 3.1 copy-start.3
  496.2 17.2 %copy-start.2 = (f32[8,896,128]{2,0,1:T(8,128)}, f32[8,896,128]{2,0,1:T(8,128)S(1)}, u32[]{:S(2)}) copy-start(f32[8,896,128]{2,0,1:T(8,128)S(1)} %broadcast_divide_fusion) | copy-start | bytes 11010052
Sparse Core Ops, SparseCore 0:
  418.9 74.1 all-reduce.1
where the time goes:
time: 569 us; the launch traced here: 568 us
  blocking collectives  243 us (43%)
  matrix products  152 us (27%)
  waiting for transfers between devices  67.3 us (12%)
  local copies, waits for them, and re-layouts  50.3 us (9%)
  other arithmetic  38.6 us (7%)
  between operations  16.7 us (3%)
    psum x12, blocking collectives, advance(): usage = lax.psum(partial_use, 'veh')  203 us
    dot_general x12, matrix products, advance(): jnp.einsum('svi,sij->svj', rounded, hessian, preferred_element_type=jnp.f...  70.6 us
    psum x1, waiting for transfers between devices, shards(): totals = lax.psum(partial_sums, 'scen')  67.3 us
    psum x1, blocking collectives, shards(): spread_total = lax.psum(spread, ('scen', 'veh'))  39.5 us
    while x36, local copies, waits for them, and re-layouts  37.1 us
    reduce_sum x12, other arithmetic, advance(): consumed = jnp.sum(roster * coefficient[None], axis=2)  25.1 us
    dot_general x1, matrix products, shards(): jnp.einsum('sb,bvi->svi', selector.astype(jnp.bfloat16), anchor, preferre...  22.6 us
    dot_general x1, matrix products, shards(): jnp.einsum('sb,bvi->svi', selector, every_mean, precision=highest)  17.2 us
  transfers between devices with their start and end apart: 1, of which 1 were waited for; matrix products, arithmetic and copies ran while one was open for 1% of the time, Pallas kernels for 0%

commit v1 on v0

--- a/solution.py
+++ b/solution.py
@@ -8,6 +8,16 @@
 step_size = 0.02
 dual_step = 0.02
 highest = lax.Precision.HIGHEST
+
+
+def make_outputs(incoming_x):
+    n_lanes = lax.axis_size("veh")
+    n_now = incoming_x
+    for d in [
+        [(src_i, src_i ^ i0) for src_i in range(n_lanes)] for i0 in (1, 2, 4, 8, 16) if i0 < n_lanes
+    ]:
+        n_now = n_now + lax.ppermute(n_now, axis_name="veh", perm=d)
+    return n_now
 
 
 def shards(
@@ -47,7 +57,7 @@
         curvature = jnp.einsum("svi,sij->svj", rounded, hessian, preferred_element_type=jnp.float32)
         consumed = jnp.sum(roster * coefficient[None], axis=2)
         partial_use = jnp.dot(consumed, crew_map, precision=highest)
-        usage = lax.psum(partial_use, "veh")
+        usage = make_outputs(partial_use)
         updated = jnp.maximum(multiplier + dual_step * (usage - crew_limit), 0.0)
         per_vehicle = jnp.dot(multiplier, crew_map.T, precision=highest)
         gradient = (

time: 569 us -> 417 us (0.73)
  blocking collectives: 243 us -> 39.5 us
  starting transfers between devices: 0.04 us -> 40 us
  waiting for transfers between devices: 67.3 us -> 78.8 us
    psum x12 -> x0, blocking collectives: 203 us -> none  [advance(): usage = lax.psum(partial_use, 'veh')]
    ppermute x0 -> x24, starting transfers between devices: none -> 40 us  [make_outputs(): n_now = n_now + lax.ppermute(n_now, axis_name='veh', perm=d)]
    ppermute x0 -> x24, waiting for transfers between devices: none -> 9.2 us  [make_outputs(): n_now = n_now + lax.ppermute(n_now, axis_name='veh', perm=d)]
  transfers between devices with their start and end apart: 1 -> 25, of which waited for: 1 -> 13; matrix products, arithmetic and copies ran while one was open for 1% -> 22% of each run, Pallas kernels for 0% -> 0%
where the time goes in v1:
time: 417 us; the launch traced here: 416 us
  matrix products  152 us (36%)
  waiting for transfers between devices  78.8 us (19%)
  local copies, waits for them, and re-layouts  50.3 us (12%)
  starting transfers between devices  40 us (10%)
  blocking collectives  39.5 us (9%)
  other arithmetic  38.6 us (9%)
  between operations  16.7 us (4%)
    dot_general x12, matrix products, advance(): jnp.einsum('svi,sij->svj', rounded, hessian, preferred_element_type=jnp.f...  70.3 us
    psum x1, waiting for transfers between devices, shards(): totals = lax.psum(partial_sums, 'scen')  69.6 us
    ppermute x24, starting transfers between devices, make_outputs(): n_now = n_now + lax.ppermute(n_now, axis_name='veh', perm=d)  40 us
    psum x1, blocking collectives, shards(): spread_total = lax.psum(spread, ('scen', 'veh'))  39.5 us
    while x36, local copies, waits for them, and re-layouts  37.1 us
    reduce_sum x12, other arithmetic, advance(): consumed = jnp.sum(roster * coefficient[None], axis=2)  25.1 us
    dot_general x1, matrix products, shards(): jnp.einsum('sb,bvi->svi', selector.astype(jnp.bfloat16), anchor, preferre...  22.6 us
    dot_general x1, matrix products, shards(): jnp.einsum('sb,bvi->svi', selector, every_mean, precision=highest)  17.2 us
  transfers between devices with their start and end apart: 25, of which 13 were waited for; matrix products, arithmetic and copies ran while one was open for 22% of the time, Pallas kernels for 0%

profile of v1, /device:TPU:0, one launch (start us, length us, event | category | flops | bytes accessed | tf_op | source)
XLA Modules:
  0.0 416.3 jit_solution(16136138179437869728)
XLA Ops:
  8.7 22.6 %fusion.12 = f32[16,896,128]{2,0,1:T(8,128)S(1)} fusion(bf16[16,896,128]{2,1,0:T(8,128)(2,1)} %param.14, bf16[16,896,128]{2,1,0:T(8,128)(2,1)} %param.15, bf16[8,896,128]{2,1,0:T(8,128)(2,1)S(1)} %copy-done, s32[16]{0:T(128)S(1)} %dynamic-slice_bitcast_fusion), kind=kOutput, calls=%fused_computation.15 | convolution fusion | flops 36700544 | bytes 16515136 | tf_op jit(solution)/shard_map/sb,bvi->svi/dot_general | solution.py:45
  31.3 5.2 %copy.27 = f32[16,896,128]{2,1,0:T(8,128)} copy(f32[16,896,128]{2,0,1:T(8,128)S(1)} %fusion.12) | data formatting | bytes 14680064
  36.5 3.8 convert_element_type.42
  40.4 210.0 %while.13 = (s32[]{:T(128)}, f32[16,896,128]{2,1,0:T(8,128)}, f32[16,350]{1,0:T(8,128)S(1)}, bf16[16,128,128]{2,1,0:T(8,128)(2,1)S(1)}, f32[16,896,128]{2,1,0:T(...) while((s32[]{:T(128)}, f32[16,896,128]{2,1,0:T(8,128)}, ...), condition=%wide.region_2.0_spmd.clone, body=%wide.region_0.0_spmd.clone.sunk | while | flops 607973248 | bytes 75482056 | solution.py:68
  40.5 3.1 copy.53
  43.5 2.1 multiply_reduce_fusion.4
  46.6 3.1 collective-permute-start
  51.5 3.0 collective-permute-start.1
  54.6 5.9 %multiply_subtract_fusion.2 = f32[16,896,128]{2,1,0:T(8,128)} fusion(f32[16,896,128]{2,1,0:T(8,128)S(1)} %copy.53, f32[16,896,128]{2,1,0:T(8,128)S(1)} %copy-done.1, f32[896,128]{1,0:T(8,128)S(1)} %get-tuple-element.185, f32[16,896]{1,0:T(8,128)S(1)} %fusion.47, bf16[16,128,128]{2,1,0:T(8,128)(2,1)S(1)} %get-tuple-element.183), kind=kOutput, calls=%fused_computation.2.clone.1 | convolution fusion | flops 482607104 | bytes 23060480 | tf_op jit(solution)/shard_map/while/body/eval_jaxpr/svi,sij->svj/dot_general | solution.py:57
  60.4 3.1 copy.53
  63.5 2.1 multiply_reduce_fusion.4
  70.5 5.9 %multiply_subtract_fusion.2 = f32[16,896,128]{2,1,0:T(8,128)} fusion(f32[16,896,128]{2,1,0:T(8,128)S(1)} %copy.53, f32[16,896,128]{2,1,0:T(8,128)S(1)} %copy-done.1, f32[896,128]{1,0:T(8,128)S(1)} %get-tuple-element.185, f32[16,896]{1,0:T(8,128)S(1)} %fusion.47, bf16[16,128,128]{2,1,0:T(8,128)(2,1)S(1)} %get-tuple-element.183), kind=kOutput, calls=%fused_computation.2.clone.1 | convolution fusion | flops 482607104 | bytes 23060480 | tf_op jit(solution)/shard_map/while/body/eval_jaxpr/svi,sij->svj/dot_general | solution.py:57
  76.4 3.1 copy.53
  86.7 2.6 collective-permute-start.1
  89.3 5.9 %multiply_subtract_fusion.2 = f32[16,896,128]{2,1,0:T(8,128)} fusion(f32[16,896,128]{2,1,0:T(8,128)S(1)} %copy.53, f32[16,896,128]{2,1,0:T(8,128)S(1)} %copy-done.1, f32[896,128]{1,0:T(8,128)S(1)} %get-tuple-element.185, f32[16,896]{1,0:T(8,128)S(1)} %fusion.47, bf16[16,128,128]{2,1,0:T(8,128)(2,1)S(1)} %get-tuple-element.183), kind=kOutput, calls=%fused_computation.2.clone.1 | convolution fusion | flops 482607104 | bytes 23060480 | tf_op jit(solution)/shard_map/while/body/eval_jaxpr/svi,sij->svj/dot_general | solution.py:57
  95.2 3.1 copy.53
  98.3 2.1 multiply_reduce_fusion.4
  105.5 5.9 %multiply_subtract_fusion.2 = f32[16,896,128]{2,1,0:T(8,128)} fusion(f32[16,896,128]{2,1,0:T(8,128)S(1)} %copy.53, f32[16,896,128]{2,1,0:T(8,128)S(1)} %copy-done.1, f32[896,128]{1,0:T(8,128)S(1)} %get-tuple-element.185, f32[16,896]{1,0:T(8,128)S(1)} %fusion.47, bf16[16,128,128]{2,1,0:T(8,128)(2,1)S(1)} %get-tuple-element.183), kind=kOutput, calls=%fused_computation.2.clone.1 | convolution fusion | flops 482607104 | bytes 23060480 | tf_op jit(solution)/shard_map/while/body/eval_jaxpr/svi,sij->svj/dot_general | solution.py:57
  111.4 3.1 copy.53
  114.5 2.1 multiply_reduce_fusion.4
  121.4 2.6 collective-permute-start.1
  124.1 5.9 %multiply_subtract_fusion.2 = f32[16,896,128]{2,1,0:T(8,128)} fusion(f32[16,896,128]{2,1,0:T(8,128)S(1)} %copy.53, f32[16,896,128]{2,1,0:T(8,128)S(1)} %copy-done.1, f32[896,128]{1,0:T(8,128)S(1)} %get-tuple-element.185, f32[16,896]{1,0:T(8,128)S(1)} %fusion.47, bf16[16,128,128]{2,1,0:T(8,128)(2,1)S(1)} %get-tuple-element.183), kind=kOutput, calls=%fused_computation.2.clone.1 | convolution fusion | flops 482607104 | bytes 23060480 | tf_op jit(solution)/shard_map/while/body/eval_jaxpr/svi,sij->svj/dot_general | solution.py:57
  130.0 3.1 copy.53
  133.1 2.1 multiply_reduce_fusion.4
  140.3 5.9 %multiply_subtract_fusion.2 = f32[16,896,128]{2,1,0:T(8,128)} fusion(f32[16,896,128]{2,1,0:T(8,128)S(1)} %copy.53, f32[16,896,128]{2,1,0:T(8,128)S(1)} %copy-done.1, f32[896,128]{1,0:T(8,128)S(1)} %get-tuple-element.185, f32[16,896]{1,0:T(8,128)S(1)} %fusion.47, bf16[16,128,128]{2,1,0:T(8,128)(2,1)S(1)} %get-tuple-element.183), kind=kOutput, calls=%fused_computation.2.clone.1 | convolution fusion | flops 482607104 | bytes 23060480 | tf_op jit(solution)/shard_map/while/body/eval_jaxpr/svi,sij->svj/dot_general | solution.py:57
  146.2 3.1 copy.53
  156.2 2.6 collective-permute-start.1
  158.9 5.9 %multiply_subtract_fusion.2 = f32[16,896,128]{2,1,0:T(8,128)} fusion(f32[16,896,128]{2,1,0:T(8,128)S(1)} %copy.53, f32[16,896,128]{2,1,0:T(8,128)S(1)} %copy-done.1, f32[896,128]{1,0:T(8,128)S(1)} %get-tuple-element.185, f32[16,896]{1,0:T(8,128)S(1)} %fusion.47, bf16[16,128,128]{2,1,0:T(8,128)(2,1)S(1)} %get-tuple-element.183), kind=kOutput, calls=%fused_computation.2.clone.1 | convolution fusion | flops 482607104 | bytes 23060480 | tf_op jit(solution)/shard_map/while/body/eval_jaxpr/svi,sij->svj/dot_general | solution.py:57
  164.7 3.1 copy.53
  175.1 5.9 %multiply_subtract_fusion.2 = f32[16,896,128]{2,1,0:T(8,128)} fusion(f32[16,896,128]{2,1,0:T(8,128)S(1)} %copy.53, f32[16,896,128]{2,1,0:T(8,128)S(1)} %copy-done.1, f32[896,128]{1,0:T(8,128)S(1)} %get-tuple-element.185, f32[16,896]{1,0:T(8,128)S(1)} %fusion.47, bf16[16,128,128]{2,1,0:T(8,128)(2,1)S(1)} %get-tuple-element.183), kind=kOutput, calls=%fused_computation.2.clone.1 | convolution fusion | flops 482607104 | bytes 23060480 | tf_op jit(solution)/shard_map/while/body/eval_jaxpr/svi,sij->svj/dot_general | solution.py:57
  180.9 3.1 copy.53
  191.0 2.6 collective-permute-start.1
  193.6 5.9 %multiply_subtract_fusion.2 = f32[16,896,128]{2,1,0:T(8,128)} fusion(f32[16,896,128]{2,1,0:T(8,128)S(1)} %copy.53, f32[16,896,128]{2,1,0:T(8,128)S(1)} %copy-done.1, f32[896,128]{1,0:T(8,128)S(1)} %get-tuple-element.185, f32[16,896]{1,0:T(8,128)S(1)} %fusion.47, bf16[16,128,128]{2,1,0:T(8,128)(2,1)S(1)} %get-tuple-element.183), kind=kOutput, calls=%fused_computation.2.clone.1 | convolution fusion | flops 482607104 | bytes 23060480 | tf_op jit(solution)/shard_map/while/body/eval_jaxpr/svi,sij->svj/dot_general | solution.py:57
  199.5 3.1 copy.53
  209.8 5.9 %multiply_subtract_fusion.2 = f32[16,896,128]{2,1,0:T(8,128)} fusion(f32[16,896,128]{2,1,0:T(8,128)S(1)} %copy.53, f32[16,896,128]{2,1,0:T(8,128)S(1)} %copy-done.1, f32[896,128]{1,0:T(8,128)S(1)} %get-tuple-element.185, f32[16,896]{1,0:T(8,128)S(1)} %fusion.47, bf16[16,128,128]{2,1,0:T(8,128)(2,1)S(1)} %get-tuple-element.183), kind=kOutput, calls=%fused_computation.2.clone.1 | convolution fusion | flops 482607104 | bytes 23060480 | tf_op jit(solution)/shard_map/while/body/eval_jaxpr/svi,sij->svj/dot_general | solution.py:57
  215.7 3.1 copy.53
  225.7 2.7 collective-permute-start.1
  228.5 5.9 %multiply_subtract_fusion.2 = f32[16,896,128]{2,1,0:T(8,128)} fusion(f32[16,896,128]{2,1,0:T(8,128)S(1)} %copy.53, f32[16,896,128]{2,1,0:T(8,128)S(1)} %copy-done.1, f32[896,128]{1,0:T(8,128)S(1)} %get-tuple-element.185, f32[16,896]{1,0:T(8,128)S(1)} %fusion.47, bf16[16,128,128]{2,1,0:T(8,128)(2,1)S(1)} %get-tuple-element.183), kind=kOutput, calls=%fused_computation.2.clone.1 | convolution fusion | flops 482607104 | bytes 23060480 | tf_op jit(solution)/shard_map/while/body/eval_jaxpr/svi,sij->svj/dot_general | solution.py:57
  234.4 3.1 copy.53
  244.6 5.9 %multiply_subtract_fusion.2 = f32[16,896,128]{2,1,0:T(8,128)} fusion(f32[16,896,128]{2,1,0:T(8,128)S(1)} %copy.53, f32[16,896,128]{2,1,0:T(8,128)S(1)} %copy-done.1, f32[896,128]{1,0:T(8,128)S(1)} %get-tuple-element.185, f32[16,896]{1,0:T(8,128)S(1)} %fusion.47, bf16[16,128,128]{2,1,0:T(8,128)(2,1)S(1)} %get-tuple-element.183), kind=kOutput, calls=%fused_computation.2.clone.1 | convolution fusion | flops 482607104 | bytes 23060480 | tf_op jit(solution)/shard_map/while/body/eval_jaxpr/svi,sij->svj/dot_general | solution.py:57
  250.5 14.0 %fusion.14 = f32[8,896,128]{2,0,1:T(8,128)} fusion(f32[16,896,128]{2,1,0:T(8,128)} %get-tuple-element.48, f32[16]{0:T(128)S(1)} %dynamic-slice_convert_fusion.1, s32[16]{0:T(128)S(1)} %dynamic-slice_bitcast_fusion), kind=kOutput, calls=%fused_computation.18 | convolution fusion | flops 176161024 | bytes 11010176 | tf_op jit(solution)/shard_map/sb,svi->bvi/dot_general | solution.py:79
  264.6 5.6 %convert_element_type.49 = bf16[16,896,128]{2,1,0:T(8,128)(2,1)} convert(f32[16,896,128]{2,1,0:T(8,128)} %get-tuple-element.48) | non-fusion elementwise | flops 1835008 | bytes 11010048 | tf_op jit(solution)/shard_map/convert_element_type | solution.py:90
  271.5 69.6 %all-reduce.2.cloned.1.call-done = f32[8,896,128]{2,0,1:T(8,128)} async-done(((f32[8,896,128]{2,0,1:T(8,128)}), f32[8,896,128]{2,0,1:T(8,128)}) %all-reduce.2.cloned.1.call-update) | async-done | bytes 3670032 | tf_op jit(solution)/shard_map/psum | solution.py:80
  341.1 2.5 broadcast_divide_fusion
  344.3 17.2 %multiply_reduce_fusion.1 = (f32[16]{0:T(128)S(1)}, bf16[16,896,128]{2,0,1:T(8,128)(2,1)S(1)}) fusion(bf16[16,896,128]{2,1,0:T(8,128)(2,1)S(1)} %copy-done.3, f32[8,896,128]{2,0,1:T(8,128)S(1)} %broadcast_divide_fusion, s32[16]{0:T(128)S(1)} %dynamic-slice_bitcast_fusion, f32[16,896,128]{2,1,0:T(8,128)} %get-tuple-element.48), kind=kOutput, calls=%fused_computation.17 | convolution fusion | flops 187170928 | bytes 18350208 | tf_op jit(solution)/shard_map/sb,bvi->svi/dot_general | solution.py:83
  362.1 2.8 copy.30
  364.9 39.5 %psum.15 = f32[]{:T(128)} all-reduce(f32[]{:T(128)} %multiply_reduce_fusion.2), channel_id=1, replica_groups=mesh['scen'=8,'veh'=4] {'scen','veh'}, use_global_device_ids=true, to_apply=%region_7.0 | all-reduce | flops 1 | bytes 8 | tf_op jit(solution)/shard_map/psum | solution.py:87
  405.2 2.4 dynamic-slice_convert_fusion
  (154 shorter events, 76.9 us)
Async XLA Ops:
  7.2 334.0 %all-reduce.2.cloned.1.call-start = ((), (), s32[]{:S(2)}) async-start(), calls=%async_computation | async-start | bytes 7340032 | tf_op jit(solution)/shard_map/psum | solution.py:80
  31.3 5.2 %copy-start.5 = (bf16[16,896,128]{2,1,0:T(8,128)(2,1)S(1)}, bf16[16,896,128]{2,1,0:T(8,128)(2,1)}, u32[]{:S(2)}) copy-start(bf16[16,896,128]{2,1,0:T(8,128)(2,1)} %param.13) | copy-start | bytes 11010052
  36.5 3.8 copy-start.9
  36.5 3.9 copy-start.10
  36.5 3.9 copy-start.4
  36.5 3.9 copy-start.7
  36.5 3.9 copy-start.8
  36.5 3.9 copy-start.11
  43.5 11.0 %copy-start.1 = (f32[16,896,128]{2,1,0:T(8,128)S(1)}, f32[16,896,128]{2,1,0:T(8,128)}, u32[]{:S(2)}) copy-start(f32[16,896,128]{2,1,0:T(8,128)} %get-tuple-element.184) | copy-start | bytes 22020100 | tf_op jit(solution)/shard_map/while
  46.6 4.9 %collective-permute-start = (f32[16,350]{1,0:T(8,128)S(1)}, f32[16,350]{1,0:T(8,128)S(1)}, u32[]{:S(2)}, u32[]{:S(2)}) collective-permute-start(f32[16,350]{1,0:T(8,128)S(1)} %fusion.48), channel_id=1, source_target_pairs={{0,1},{1,0},{2,3},{3,2},{4,5},{5,4},{6,7},{7,6},{8,9},{9,8},{10,11... | collective-permute-start | bytes 67208 | tf_op jit(solution)/shard_map/while/body/eval_jaxpr/ppermute | solution.py:19
  51.5 8.9 %collective-permute-start.1 = (f32[16,350]{1,0:T(8,128)S(1)}, f32[16,350]{1,0:T(8,128)S(1)}, u32[]{:S(2)}, u32[]{:S(2)}) collective-permute-start(f32[16,350]{1,0:T(8,128)S(1)} %add.73), channel_id=1, source_target_pairs={{0,2},{1,3},{2,0},{3,1},{4,6},{5,7},{6,4},{7,5},{8,10},{9,11},{10,... | collective-permute-start | bytes 67208 | tf_op jit(solution)/shard_map/while/body/eval_jaxpr/ppermute | solution.py:19
  63.5 7.0 %copy-start.1 = (f32[16,896,128]{2,1,0:T(8,128)S(1)}, f32[16,896,128]{2,1,0:T(8,128)}, u32[]{:S(2)}) copy-start(f32[16,896,128]{2,1,0:T(8,128)} %get-tuple-element.184) | copy-start | bytes 22020100 | tf_op jit(solution)/shard_map/while
  66.6 3.9 collective-permute-start
  70.5 5.9 %collective-permute-start.1 = (f32[16,350]{1,0:T(8,128)S(1)}, f32[16,350]{1,0:T(8,128)S(1)}, u32[]{:S(2)}, u32[]{:S(2)}) collective-permute-start(f32[16,350]{1,0:T(8,128)S(1)} %add.73), channel_id=1, source_target_pairs={{0,2},{1,3},{2,0},{3,1},{4,6},{5,7},{6,4},{7,5},{8,10},{9,11},{10,... | collective-permute-start | bytes 67208 | tf_op jit(solution)/shard_map/while/body/eval_jaxpr/ppermute | solution.py:19
  79.5 9.8 %copy-start.1 = (f32[16,896,128]{2,1,0:T(8,128)S(1)}, f32[16,896,128]{2,1,0:T(8,128)}, u32[]{:S(2)}) copy-start(f32[16,896,128]{2,1,0:T(8,128)} %get-tuple-element.184) | copy-start | bytes 22020100 | tf_op jit(solution)/shard_map/while
  82.5 4.1 collective-permute-start
  86.7 8.5 %collective-permute-start.1 = (f32[16,350]{1,0:T(8,128)S(1)}, f32[16,350]{1,0:T(8,128)S(1)}, u32[]{:S(2)}, u32[]{:S(2)}) collective-permute-start(f32[16,350]{1,0:T(8,128)S(1)} %add.73), channel_id=1, source_target_pairs={{0,2},{1,3},{2,0},{3,1},{4,6},{5,7},{6,4},{7,5},{8,10},{9,11},{10,... | collective-permute-start | bytes 67208 | tf_op jit(solution)/shard_map/while/body/eval_jaxpr/ppermute | solution.py:19
  98.3 7.2 %copy-start.1 = (f32[16,896,128]{2,1,0:T(8,128)S(1)}, f32[16,896,128]{2,1,0:T(8,128)}, u32[]{:S(2)}) copy-start(f32[16,896,128]{2,1,0:T(8,128)} %get-tuple-element.184) | copy-start | bytes 22020100 | tf_op jit(solution)/shard_map/while
  101.3 3.9 collective-permute-start
  105.2 6.1 %collective-permute-start.1 = (f32[16,350]{1,0:T(8,128)S(1)}, f32[16,350]{1,0:T(8,128)S(1)}, u32[]{:S(2)}, u32[]{:S(2)}) collective-permute-start(f32[16,350]{1,0:T(8,128)S(1)} %add.73), channel_id=1, source_target_pairs={{0,2},{1,3},{2,0},{3,1},{4,6},{5,7},{6,4},{7,5},{8,10},{9,11},{10,... | collective-permute-start | bytes 67208 | tf_op jit(solution)/shard_map/while/body/eval_jaxpr/ppermute | solution.py:19
  114.5 9.6 %copy-start.1 = (f32[16,896,128]{2,1,0:T(8,128)S(1)}, f32[16,896,128]{2,1,0:T(8,128)}, u32[]{:S(2)}) copy-start(f32[16,896,128]{2,1,0:T(8,128)} %get-tuple-element.184) | copy-start | bytes 22020100 | tf_op jit(solution)/shard_map/while
  117.5 3.9 collective-permute-start
  121.4 8.5 %collective-permute-start.1 = (f32[16,350]{1,0:T(8,128)S(1)}, f32[16,350]{1,0:T(8,128)S(1)}, u32[]{:S(2)}, u32[]{:S(2)}) collective-permute-start(f32[16,350]{1,0:T(8,128)S(1)} %add.73), channel_id=1, source_target_pairs={{0,2},{1,3},{2,0},{3,1},{4,6},{5,7},{6,4},{7,5},{8,10},{9,11},{10,... | collective-permute-start | bytes 67208 | tf_op jit(solution)/shard_map/while/body/eval_jaxpr/ppermute | solution.py:19
  133.1 7.2 %copy-start.1 = (f32[16,896,128]{2,1,0:T(8,128)S(1)}, f32[16,896,128]{2,1,0:T(8,128)}, u32[]{:S(2)}) copy-start(f32[16,896,128]{2,1,0:T(8,128)} %get-tuple-element.184) | copy-start | bytes 22020100 | tf_op jit(solution)/shard_map/while
  136.1 3.9 collective-permute-start
  140.0 6.1 %collective-permute-start.1 = (f32[16,350]{1,0:T(8,128)S(1)}, f32[16,350]{1,0:T(8,128)S(1)}, u32[]{:S(2)}, u32[]{:S(2)}) collective-permute-start(f32[16,350]{1,0:T(8,128)S(1)} %add.73), channel_id=1, source_target_pairs={{0,2},{1,3},{2,0},{3,1},{4,6},{5,7},{6,4},{7,5},{8,10},{9,11},{10,... | collective-permute-start | bytes 67208 | tf_op jit(solution)/shard_map/while/body/eval_jaxpr/ppermute | solution.py:19
  149.3 9.6 %copy-start.1 = (f32[16,896,128]{2,1,0:T(8,128)S(1)}, f32[16,896,128]{2,1,0:T(8,128)}, u32[]{:S(2)}) copy-start(f32[16,896,128]{2,1,0:T(8,128)} %get-tuple-element.184) | copy-start | bytes 22020100 | tf_op jit(solution)/shard_map/while
  152.3 3.9 collective-permute-start
  156.2 8.5 %collective-permute-start.1 = (f32[16,350]{1,0:T(8,128)S(1)}, f32[16,350]{1,0:T(8,128)S(1)}, u32[]{:S(2)}, u32[]{:S(2)}) collective-permute-start(f32[16,350]{1,0:T(8,128)S(1)} %add.73), channel_id=1, source_target_pairs={{0,2},{1,3},{2,0},{3,1},{4,6},{5,7},{6,4},{7,5},{8,10},{9,11},{10,... | collective-permute-start | bytes 67208 | tf_op jit(solution)/shard_map/while/body/eval_jaxpr/ppermute | solution.py:19
  167.8 7.2 %copy-start.1 = (f32[16,896,128]{2,1,0:T(8,128)S(1)}, f32[16,896,128]{2,1,0:T(8,128)}, u32[]{:S(2)}) copy-start(f32[16,896,128]{2,1,0:T(8,128)} %get-tuple-element.184) | copy-start | bytes 22020100 | tf_op jit(solution)/shard_map/while
  170.9 3.9 collective-permute-start
  174.8 6.1 %collective-permute-start.1 = (f32[16,350]{1,0:T(8,128)S(1)}, f32[16,350]{1,0:T(8,128)S(1)}, u32[]{:S(2)}, u32[]{:S(2)}) collective-permute-start(f32[16,350]{1,0:T(8,128)S(1)} %add.73), channel_id=1, source_target_pairs={{0,2},{1,3},{2,0},{3,1},{4,6},{5,7},{6,4},{7,5},{8,10},{9,11},{10,... | collective-permute-start | bytes 67208 | tf_op jit(solution)/shard_map/while/body/eval_jaxpr/ppermute | solution.py:19
  184.0 9.6 %copy-start.1 = (f32[16,896,128]{2,1,0:T(8,128)S(1)}, f32[16,896,128]{2,1,0:T(8,128)}, u32[]{:S(2)}) copy-start(f32[16,896,128]{2,1,0:T(8,128)} %get-tuple-element.184) | copy-start | bytes 22020100 | tf_op jit(solution)/shard_map/while
  187.1 3.9 collective-permute-start
  191.0 8.5 %collective-permute-start.1 = (f32[16,350]{1,0:T(8,128)S(1)}, f32[16,350]{1,0:T(8,128)S(1)}, u32[]{:S(2)}, u32[]{:S(2)}) collective-permute-start(f32[16,350]{1,0:T(8,128)S(1)} %add.73), channel_id=1, source_target_pairs={{0,2},{1,3},{2,0},{3,1},{4,6},{5,7},{6,4},{7,5},{8,10},{9,11},{10,... | collective-permute-start | bytes 67208 | tf_op jit(solution)/shard_map/while/body/eval_jaxpr/ppermute | solution.py:19
  202.6 7.2 %copy-start.1 = (f32[16,896,128]{2,1,0:T(8,128)S(1)}, f32[16,896,128]{2,1,0:T(8,128)}, u32[]{:S(2)}) copy-start(f32[16,896,128]{2,1,0:T(8,128)} %get-tuple-element.184) | copy-start | bytes 22020100 | tf_op jit(solution)/shard_map/while
  205.6 3.9 collective-permute-start
  209.5 6.1 %collective-permute-start.1 = (f32[16,350]{1,0:T(8,128)S(1)}, f32[16,350]{1,0:T(8,128)S(1)}, u32[]{:S(2)}, u32[]{:S(2)}) collective-permute-start(f32[16,350]{1,0:T(8,128)S(1)} %add.73), channel_id=1, source_target_pairs={{0,2},{1,3},{2,0},{3,1},{4,6},{5,7},{6,4},{7,5},{8,10},{9,11},{10,... | collective-permute-start | bytes 67208 | tf_op jit(solution)/shard_map/while/body/eval_jaxpr/ppermute | solution.py:19
  218.8 9.7 %copy-start.1 = (f32[16,896,128]{2,1,0:T(8,128)S(1)}, f32[16,896,128]{2,1,0:T(8,128)}, u32[]{:S(2)}) copy-start(f32[16,896,128]{2,1,0:T(8,128)} %get-tuple-element.184) | copy-start | bytes 22020100 | tf_op jit(solution)/shard_map/while
  221.8 3.9 collective-permute-start
  225.7 8.6 %collective-permute-start.1 = (f32[16,350]{1,0:T(8,128)S(1)}, f32[16,350]{1,0:T(8,128)S(1)}, u32[]{:S(2)}, u32[]{:S(2)}) collective-permute-start(f32[16,350]{1,0:T(8,128)S(1)} %add.73), channel_id=1, source_target_pairs={{0,2},{1,3},{2,0},{3,1},{4,6},{5,7},{6,4},{7,5},{8,10},{9,11},{10,... | collective-permute-start | bytes 67208 | tf_op jit(solution)/shard_map/while/body/eval_jaxpr/ppermute | solution.py:19
  237.5 7.1 %copy-start.1 = (f32[16,896,128]{2,1,0:T(8,128)S(1)}, f32[16,896,128]{2,1,0:T(8,128)}, u32[]{:S(2)}) copy-start(f32[16,896,128]{2,1,0:T(8,128)} %get-tuple-element.184) | copy-start | bytes 22020100 | tf_op jit(solution)/shard_map/while
  240.5 3.9 collective-permute-start
  244.4 6.0 %collective-permute-start.1 = (f32[16,350]{1,0:T(8,128)S(1)}, f32[16,350]{1,0:T(8,128)S(1)}, u32[]{:S(2)}, u32[]{:S(2)}) collective-permute-start(f32[16,350]{1,0:T(8,128)S(1)} %add.73), channel_id=1, source_target_pairs={{0,2},{1,3},{2,0},{3,1},{4,6},{5,7},{6,4},{7,5},{8,10},{9,11},{10,... | collective-permute-start | bytes 67208 | tf_op jit(solution)/shard_map/while/body/eval_jaxpr/ppermute | solution.py:19
  250.5 14.1 %copy-start.6 = (f32[16,350]{1,0:T(8,128)}, f32[16,350]{1,0:T(8,128)S(1)}, u32[]{:S(2)}) copy-start(f32[16,350]{1,0:T(8,128)S(1)} %get-tuple-element.93) | copy-start | bytes 67204
  264.5 6.9 %copy-start.12 = (s32[128,1]{0,1:T(1,128)S(1)}, s32[128,1]{0,1:T(1,128)}, u32[]{:S(2)}) copy-start(s32[128,1]{0,1:T(1,128)} %param.22) | copy-start | bytes 1540
  341.1 3.1 copy-start.3
  344.3 17.2 %copy-start.2 = (f32[8,896,128]{2,0,1:T(8,128)}, f32[8,896,128]{2,0,1:T(8,128)S(1)}, u32[]{:S(2)}) copy-start(f32[8,896,128]{2,0,1:T(8,128)S(1)} %broadcast_divide_fusion) | copy-start | bytes 11010052
  (1 other events, 1.5 us)
Sparse Core Ops, SparseCore 0:
  264.7 76.4 all-reduce.1
